TPU v7x, 128 devices: a whole 4x4x4 slice. The times are simulated.
128 devices in a mesh: grp: 4 (over z), slab: 32 (over y, x, core).
Axes of the slice: x: 4, y: 4, z: 4, core: 2. Of those that a mesh axis runs over, the one named last changes fastest.
Arguments:
- tensor: float32 [672, 256, 672], P('grp', 'slab'), may hold values from -20 to 20
- start_one: float32 [672, 96], replicated, may hold values from -6 to 6
- start_two: float32 [672, 96], replicated, may hold values from -6 to 6
Outputs:
- basis_one: float32 [672, 96], replicated
- basis_two: float32 [672, 96], replicated
- core: float32 [96, 256, 96], P('grp', 'slab')
All inputs are finite; a program needn't handle non-finite values.
Results may differ from a plain program's by a relative error of at most 0.0003.
Values sent between devices are 32-bit elements; how exact they have to be, the bound alone decides.
A program may use at most 64 MiB of HBM per device.

v0:
```python
import jax
import jax.numpy as jnp
from jax import lax
from jax.sharding import PartitionSpec as P

ITERS = 2
HIGH = lax.Precision.HIGHEST


def orthonormal(widened):
    cross = jnp.dot(widened.T, widened, precision=HIGH)
    lower_small = jnp.linalg.cholesky(cross)
    return lax.linalg.triangular_solve(
        lower_small, widened, left_side=False, lower=True, transpose_a=True
    )


def iterate_basis(gram, start):
    current = start
    for _ in range(ITERS):
        current = orthonormal(jnp.dot(gram, current, precision=HIGH))
    return current


def local(tensor, start_one, start_two):
    block_gram = jnp.einsum("jmi,jmk->ik", tensor, tensor, precision=HIGH)
    gram_one = lax.psum(block_gram, ("grp", "slab"))
    basis_one = iterate_basis(gram_one, start_one)
    reduced = jnp.einsum("jmi,ia->jma", tensor, basis_one, precision=HIGH)
    regrouped = lax.all_to_all(reduced, "grp", split_axis=1, concat_axis=0, tiled=True)
    block_second = jnp.einsum("jma,kma->jk", regrouped, regrouped, precision=HIGH)
    gram_two = lax.psum(block_second, ("grp", "slab"))
    basis_two = iterate_basis(gram_two, start_two)
    second_rows = tensor.shape[0]
    own_basis = lax.dynamic_slice_in_dim(
        basis_two, lax.axis_index("grp") * second_rows, second_rows, 0
    )
    partial_core = jnp.einsum("jb,jma->bma", own_basis, reduced, precision=HIGH)
    core = lax.psum_scatter(partial_core, "grp", scatter_dimension=0, tiled=True)
    return (basis_one, basis_two, core)


def solution(mesh):
    in_specs = (P("grp", "slab", None), P(), P())
    out_specs = (P(), P(), P("grp", "slab", None))
    return jax.shard_map(local, mesh=mesh, in_specs=in_specs, out_specs=out_specs, check_vma=False)
```

profile of v0, /device:TPU:0, one launch (start us, length us, event | category | flops | bytes accessed | tf_op | source)
XLA Modules:
  0.0 465.3 jit_solution(15145513758969465968)
XLA Ops:
  7.2 0.0 copy-start
  7.2 0.0 all-reduce.3.cloned.1.call-start
  7.2 18.1 %fusion.4 = f32[672,672]{1,0:T(8,128)} fusion(f32[168,8,672]{2,1,0:T(8,128)} %param.6), kind=kOutput, calls=%fused_computation.5 | convolution fusion | flops 7283146752 | bytes 5419008 | tf_op jit(solution)/shard_map/jmi,jmk->ik/dot_general | solution.py:26
  25.3 0.0 all-reduce.3.cloned.1.call-update
  25.3 0.2 all-reduce.5.cloned.1.call-start
  25.6 152.5 %all-reduce.3.cloned.1.call-done = f32[672,672]{1,0:T(8,128)} async-done(((f32[672,672]{1,0:T(8,128)}), f32[672,672]{1,0:T(8,128)}) %all-reduce.3.cloned.1.call-update) | async-done | bytes 1806352 | tf_op jit(solution)/shard_map/psum | solution.py:27
  178.1 0.0 copy-done
  178.1 0.0 copy-start.2
  178.1 3.7 fusion.30
  181.8 0.4 fusion.31
  182.2 0.1 copy.18
  182.3 8.8 %cholesky.74 = f32[96,96]{1,0:T(8,128)S(1)} custom-call(f32[96,96]{1,0:T(8,128)S(1)} %fusion.26), custom_call_target="Cholesky" | custom-call | tf_op jit(solution)/shard_map/jit(cholesky)/cholesky | solution.py:12
  191.1 0.6 compare_reduce_fusion.3
  191.7 0.7 fusion.14
  192.4 7.4 %custom-call.8 = f32[1,96,96]{1,2,0:T(8,128)S(1)} custom-call(f32[1,96,96]{2,1,0:T(8,128)S(1)} %fusion.14), custom_call_target="InvertDiagBlocksLowerTriangular" | custom-call | tf_op jit(solution)/shard_map/triangular_solve/custom-call.0 | solution.py:13
  199.8 0.4 convolution_bitcast_fusion.3
  200.2 0.0 copy-done.2
  200.2 2.0 fusion.32
  202.2 0.4 fusion.33
  202.6 0.1 copy.19
  202.7 8.8 %cholesky.85 = f32[96,96]{1,0:T(8,128)S(1)} custom-call(f32[96,96]{1,0:T(8,128)S(1)} %fusion.24), custom_call_target="Cholesky" | custom-call | tf_op jit(solution)/shard_map/jit(cholesky)/cholesky | solution.py:12
  211.5 0.6 compare_reduce_fusion.2
  212.1 0.7 fusion.15
  212.8 7.4 %custom-call.9 = f32[1,96,96]{1,2,0:T(8,128)S(1)} custom-call(f32[1,96,96]{2,1,0:T(8,128)S(1)} %fusion.15), custom_call_target="InvertDiagBlocksLowerTriangular" | custom-call | tf_op jit(solution)/shard_map/triangular_solve/custom-call.0 | solution.py:13
  220.2 0.4 fusion.22
  220.6 0.0 copy-start.3
  220.6 6.5 %fusion.7 = f32[168,8,96]{2,0,1:T(8,128)S(1)} fusion(f32[168,8,672]{2,1,0:T(8,128)} %param.6, f32[96,672]{1,0:T(8,128)S(1)} %fusion.22), kind=kOutput, calls=%fused_computation.6 | convolution fusion | flops 1040449536 | bytes 4386816 | tf_op jit(solution)/shard_map/jmi,ia->jma/dot_general | solution.py:29
  227.1 0.0 copy-done.3
  227.1 15.1 %all_to_all.18 = f32[168,8,96]{2,0,1:T(8,128)S(1)} all-to-all(f32[168,8,96]{2,0,1:T(8,128)S(1)} %fusion.7), channel_id=1, replica_groups=mesh['grp'=4,'slab'=32] {'grp'}, dimensions={1} | all-to-all | bytes 1032192 | tf_op jit(solution)/shard_map/all_to_all | solution.py:30
  242.2 3.1 convolution_bitcast_fusion
  245.3 0.0 all-reduce.5.cloned.1.call-update
  245.3 0.0 reduce-scatter.2.cloned.1.call-start
  245.4 147.7 %all-reduce.5.cloned.1.call-done = f32[672,672]{1,0:T(8,128)} async-done(((f32[672,672]{1,0:T(8,128)}), f32[672,672]{1,0:T(8,128)}) %all-reduce.5.cloned.1.call-update) | async-done | bytes 1806352 | tf_op jit(solution)/shard_map/psum | solution.py:32
  393.1 0.0 copy-start.1
  393.1 3.7 fusion.34
  396.8 0.4 fusion.35
  397.2 0.1 copy.24
  397.3 8.8 %cholesky.96 = f32[96,96]{1,0:T(8,128)S(1)} custom-call(f32[96,96]{1,0:T(8,128)S(1)} %fusion.21), custom_call_target="Cholesky" | custom-call | tf_op jit(solution)/shard_map/jit(cholesky)/cholesky | solution.py:12
  406.1 0.6 compare_reduce_fusion.1
  406.7 0.7 fusion.16
  407.4 7.4 %custom-call.10 = f32[1,96,96]{1,2,0:T(8,128)S(1)} custom-call(f32[1,96,96]{2,1,0:T(8,128)S(1)} %fusion.16), custom_call_target="InvertDiagBlocksLowerTriangular" | custom-call | tf_op jit(solution)/shard_map/triangular_solve/custom-call.0 | solution.py:13
  414.8 0.4 convolution_bitcast_fusion.2
  415.2 0.0 copy-done.1
  415.2 2.0 fusion.36
  417.2 0.4 fusion.37
  417.6 0.1 copy.25
  417.7 8.8 %cholesky.107 = f32[96,96]{1,0:T(8,128)S(1)} custom-call(f32[96,96]{1,0:T(8,128)S(1)} %fusion.19), custom_call_target="Cholesky" | custom-call | tf_op jit(solution)/shard_map/jit(cholesky)/cholesky | solution.py:12
  426.5 0.6 compare_reduce_fusion
  427.2 0.7 fusion.17
  427.8 7.4 %custom-call.11 = f32[1,96,96]{1,2,0:T(8,128)S(1)} custom-call(f32[1,96,96]{2,1,0:T(8,128)S(1)} %fusion.17), custom_call_target="InvertDiagBlocksLowerTriangular" | custom-call | tf_op jit(solution)/shard_map/triangular_solve/custom-call.0 | solution.py:13
  435.2 0.4 convolution_bitcast_fusion.1
  435.6 0.0 copy-start.4
  435.7 1.3 fusion.11
  436.9 0.0 reduce-scatter.2.cloned.1.call-update
  437.0 19.9 %reduce-scatter.2.cloned.1.call-done = f32[24,8,96]{2,0,1:T(8,128)} async-done(((f32[96,8,96]{2,0,1:T(8,128)}), f32[24,8,96]{2,0,1:T(8,128)}) %reduce-scatter.2.cloned.1.call-update) | async-done | bytes 73744 | tf_op jit(solution)/shard_map/reduce_scatter | solution.py:39
  456.8 1.6 copy.27
  458.4 0.0 copy-done.4
  (9 shorter events, 0.2 us)
Async XLA Ops:
  7.2 170.9 %copy-start = (f32[672,96]{0,1:T(8,128)S(1)}, f32[672,96]{0,1:T(8,128)}, u32[]{:S(2)}) copy-start(f32[672,96]{0,1:T(8,128)} %param.7) | copy-start | bytes 774148
  7.2 170.9 %all-reduce.3.cloned.1.call-start = ((), (), s32[]{:S(2)}) async-start(), calls=%async_computation.2 | async-start | bytes 4128768 | tf_op jit(solution)/shard_map/psum | solution.py:27
  25.3 367.8 %all-reduce.5.cloned.1.call-start = ((), (), s32[]{:S(2)}) async-start(), calls=%async_computation.3 | async-start | bytes 4128768 | tf_op jit(solution)/shard_map/psum | solution.py:32
  178.1 22.1 %copy-start.2 = (f32[672,672]{1,0:T(8,128)S(1)}, f32[672,672]{1,0:T(8,128)}, u32[]{:S(2)}) copy-start(f32[672,672]{1,0:T(8,128)} %all-reduce.3.cloned.1.call-done) | copy-start | bytes 5419012
  220.6 6.5 %copy-start.3 = (f32[96,672]{1,0:T(8,128)}, f32[96,672]{1,0:T(8,128)S(1)}, u32[]{:S(2)}) copy-start(f32[96,672]{1,0:T(8,128)S(1)} %fusion.22) | copy-start | bytes 774148
  245.3 211.5 %reduce-scatter.2.cloned.1.call-start = ((), (), s32[]{:S(2)}) async-start(), calls=%async_computation.4 | async-start | bytes 491520 | tf_op jit(solution)/shard_map/reduce_scatter | solution.py:39
  393.1 22.1 %copy-start.1 = (f32[672,672]{1,0:T(8,128)S(1)}, f32[672,672]{1,0:T(8,128)}, u32[]{:S(2)}) copy-start(f32[672,672]{1,0:T(8,128)} %all-reduce.5.cloned.1.call-done) | copy-start | bytes 5419012
  435.6 22.8 %copy-start.4 = (f32[672,96]{0,1:T(8,128)}, f32[672,96]{0,1:T(8,128)S(1)}, u32[]{:S(2)}) copy-start(f32[672,96]{0,1:T(8,128)S(1)} %convolution_bitcast_fusion.1) | copy-start | bytes 774148
Sparse Core Ops, SparseCore 0:
  25.5 152.5 all-reduce.2
  245.4 147.5 all-reduce.4
  437.1 19.7 reduce-scatter.1
where the time goes:
time: 471 us; the launch traced here: 465 us
  waiting for transfers between devices  320 us (68%)
  other arithmetic  69.9 us (15%)
  matrix products  43.5 us (9%)
  blocking collectives  15.1 us (3%)
  between operations  14.4 us (3%)
    psum x1, waiting for transfers between devices, local(): gram_one = lax.psum(block_gram, ('grp', 'slab'))  153 us
    psum x1, waiting for transfers between devices, local(): gram_two = lax.psum(block_second, ('grp', 'slab'))  148 us
    another operation x12, other arithmetic, orthonormal(): lower_small = jnp.linalg.cholesky(cross)  37.8 us
    another operation x8, other arithmetic, orthonormal(): lax.linalg.triangular_solve(lower_small, widened, left_side=False, lower=...  32 us
    reduce_scatter x1, waiting for transfers between devices, local(): lax.psum_scatter(partial_core, 'grp', scatter_dimension=0, tiled=True)  19.9 us
    dot_general x1, matrix products, local(): block_gram = jnp.einsum('jmi,jmk->ik', tensor, tensor, precision=HIGH)  18.1 us
    all_to_all x1, blocking collectives, local(): lax.all_to_all(reduced, 'grp', split_axis=1, concat_axis=0, tiled=True)  15.1 us
    dot_general x4, matrix products, iterate_basis(): current = orthonormal(jnp.dot(gram, current, precision=HIGH))  11.3 us
  transfers between devices with their start and end apart: 3, of which 3 were waited for; matrix products, arithmetic and copies ran while one was open for 0% of the time, Pallas kernels for 0%

commit v1 on v0

--- a/solution.py
+++ b/solution.py
@@ -29,7 +29,7 @@
     reduced = jnp.einsum("jmi,ia->jma", tensor, basis_one, precision=HIGH)
     regrouped = lax.all_to_all(reduced, "grp", split_axis=1, concat_axis=0, tiled=True)
     block_second = jnp.einsum("jma,kma->jk", regrouped, regrouped, precision=HIGH)
-    gram_two = lax.psum(block_second, ("grp", "slab"))
+    gram_two = lax.psum(lax.psum(block_second, "slab"), "grp")
     basis_two = iterate_basis(gram_two, start_two)
     second_rows = tensor.shape[0]
     own_basis = lax.dynamic_slice_in_dim(

time: 471 us -> 490 us (1.040)
  waiting for transfers between devices: 320 us -> 339 us
    psum x1 -> x2, waiting for transfers between devices: 148 us -> 165 us  [local(): gram_two = lax.psum(lax.psum(block_second, 'slab'), 'grp')]
  transfers between devices with their start and end apart: 3 -> 4, of which waited for: 3 -> 4; matrix products, arithmetic and copies ran while one was open for 0% -> 0% of each run, Pallas kernels for 0% -> 0%
where the time goes in v1:
time: 490 us; the launch traced here: 484 us
  waiting for transfers between devices  339 us (69%)
  other arithmetic  69.9 us (14%)
  matrix products  43.6 us (9%)
  blocking collectives  15.1 us (3%)
  between operations  14.4 us (3%)
    psum x2, waiting for transfers between devices, local(): gram_two = lax.psum(lax.psum(block_second, 'slab'), 'grp')  165 us
    psum x1, waiting for transfers between devices, local(): gram_one = lax.psum(block_gram, ('grp', 'slab'))  153 us
    another operation x12, other arithmetic, orthonormal(): lower_small = jnp.linalg.cholesky(cross)  37.8 us
    another operation x8, other arithmetic, orthonormal(): lax.linalg.triangular_solve(lower_small, widened, left_side=False, lower=...  32 us
    reduce_scatter x1, waiting for transfers between devices, local(): lax.psum_scatter(partial_core, 'grp', scatter_dimension=0, tiled=True)  21 us
    dot_general x1, matrix products, local(): block_gram = jnp.einsum('jmi,jmk->ik', tensor, tensor, precision=HIGH)  18.1 us
    all_to_all x1, blocking collectives, local(): lax.all_to_all(reduced, 'grp', split_axis=1, concat_axis=0, tiled=True)  15.1 us
    dot_general x4, matrix products, iterate_basis(): current = orthonormal(jnp.dot(gram, current, precision=HIGH))  11.3 us
  transfers between devices with their start and end apart: 4, of which 4 were waited for; matrix products, arithmetic and copies ran while one was open for 0% of the time, Pallas kernels for 0%

profile of v1, /device:TPU:0, one launch (start us, length us, event | category | flops | bytes accessed | tf_op | source)
XLA Modules:
  0.0 484.2 jit_solution(2123889477987052942)
XLA Ops:
  7.2 0.0 copy-start
  7.2 0.0 all-reduce.4.cloned.1.call-start
  7.2 18.1 %fusion.4 = f32[672,672]{1,0:T(8,128)} fusion(f32[168,8,672]{2,1,0:T(8,128)} %param.6), kind=kOutput, calls=%fused_computation.5 | convolution fusion | flops 7283146752 | bytes 5419008 | tf_op jit(solution)/shard_map/jmi,jmk->ik/dot_general | solution.py:26
  25.3 0.0 all-reduce.4.cloned.1.call-update
  25.3 0.2 all-reduce.6.cloned.1.call-start
  25.6 152.5 %all-reduce.4.cloned.1.call-done = f32[672,672]{1,0:T(8,128)} async-done(((f32[672,672]{1,0:T(8,128)}), f32[672,672]{1,0:T(8,128)}) %all-reduce.4.cloned.1.call-update) | async-done | bytes 1806352 | tf_op jit(solution)/shard_map/psum | solution.py:27
  178.1 0.0 copy-done
  178.1 0.0 copy-start.2
  178.1 3.7 fusion.30
  181.8 0.4 fusion.31
  182.2 0.1 copy.18
  182.3 8.8 %cholesky.74 = f32[96,96]{1,0:T(8,128)S(1)} custom-call(f32[96,96]{1,0:T(8,128)S(1)} %fusion.26), custom_call_target="Cholesky" | custom-call | tf_op jit(solution)/shard_map/jit(cholesky)/cholesky | solution.py:12
  191.1 0.6 compare_reduce_fusion.3
  191.7 0.7 fusion.14
  192.4 7.4 %custom-call.8 = f32[1,96,96]{1,2,0:T(8,128)S(1)} custom-call(f32[1,96,96]{2,1,0:T(8,128)S(1)} %fusion.14), custom_call_target="InvertDiagBlocksLowerTriangular" | custom-call | tf_op jit(solution)/shard_map/triangular_solve/custom-call.0 | solution.py:13
  199.8 0.4 convolution_bitcast_fusion.3
  200.2 0.0 copy-done.2
  200.2 2.0 fusion.32
  202.2 0.4 fusion.33
  202.6 0.1 copy.19
  202.7 8.8 %cholesky.85 = f32[96,96]{1,0:T(8,128)S(1)} custom-call(f32[96,96]{1,0:T(8,128)S(1)} %fusion.24), custom_call_target="Cholesky" | custom-call | tf_op jit(solution)/shard_map/jit(cholesky)/cholesky | solution.py:12
  211.5 0.6 compare_reduce_fusion.2
  212.1 0.7 fusion.15
  212.8 7.4 %custom-call.9 = f32[1,96,96]{1,2,0:T(8,128)S(1)} custom-call(f32[1,96,96]{2,1,0:T(8,128)S(1)} %fusion.15), custom_call_target="InvertDiagBlocksLowerTriangular" | custom-call | tf_op jit(solution)/shard_map/triangular_solve/custom-call.0 | solution.py:13
  220.2 0.4 fusion.22
  220.6 0.0 copy-start.3
  220.6 6.5 %fusion.7 = f32[168,8,96]{2,0,1:T(8,128)S(1)} fusion(f32[168,8,672]{2,1,0:T(8,128)} %param.6, f32[96,672]{1,0:T(8,128)S(1)} %fusion.22), kind=kOutput, calls=%fused_computation.6 | convolution fusion | flops 1040449536 | bytes 4386816 | tf_op jit(solution)/shard_map/jmi,ia->jma/dot_general | solution.py:29
  227.1 0.0 copy-done.3
  227.1 15.1 %all_to_all.18 = f32[168,8,96]{2,0,1:T(8,128)S(1)} all-to-all(f32[168,8,96]{2,0,1:T(8,128)S(1)} %fusion.7), channel_id=1, replica_groups=mesh['grp'=4,'slab'=32] {'grp'}, dimensions={1} | all-to-all | bytes 1032192 | tf_op jit(solution)/shard_map/all_to_all | solution.py:30
  242.2 3.1 convolution_bitcast_fusion
  245.3 0.0 all-reduce.6.cloned.1.call-update
  245.3 0.0 all-reduce.8.cloned.1.call-start
  245.4 104.9 %all-reduce.6.cloned.1.call-done = f32[672,672]{1,0:T(8,128)} async-done(((f32[672,672]{1,0:T(8,128)}), f32[672,672]{1,0:T(8,128)}) %all-reduce.6.cloned.1.call-update) | async-done | bytes 1806352 | tf_op jit(solution)/shard_map/psum | solution.py:32
  350.2 0.0 all-reduce.8.cloned.1.call-update
  350.3 0.0 reduce-scatter.2.cloned.1.call-start
  350.3 60.5 %all-reduce.8.cloned.1.call-done = f32[672,672]{1,0:T(8,128)} async-done(((f32[672,672]{1,0:T(8,128)}), f32[672,672]{1,0:T(8,128)}) %all-reduce.8.cloned.1.call-update) | async-done | bytes 1806352 | tf_op jit(solution)/shard_map/psum | solution.py:32
  410.8 0.0 copy-start.1
  410.8 3.7 fusion.34
  414.5 0.4 fusion.35
  414.9 0.1 copy.24
  415.0 8.8 %cholesky.96 = f32[96,96]{1,0:T(8,128)S(1)} custom-call(f32[96,96]{1,0:T(8,128)S(1)} %fusion.21), custom_call_target="Cholesky" | custom-call | tf_op jit(solution)/shard_map/jit(cholesky)/cholesky | solution.py:12
  423.9 0.6 compare_reduce_fusion.1
  424.5 0.7 fusion.16
  425.2 7.4 %custom-call.10 = f32[1,96,96]{1,2,0:T(8,128)S(1)} custom-call(f32[1,96,96]{2,1,0:T(8,128)S(1)} %fusion.16), custom_call_target="InvertDiagBlocksLowerTriangular" | custom-call | tf_op jit(solution)/shard_map/triangular_solve/custom-call.0 | solution.py:13
  432.5 0.4 convolution_bitcast_fusion.2
  433.0 0.0 copy-done.1
  433.0 2.0 fusion.36
  435.0 0.4 fusion.37
  435.4 0.1 copy.25
  435.5 8.8 %cholesky.107 = f32[96,96]{1,0:T(8,128)S(1)} custom-call(f32[96,96]{1,0:T(8,128)S(1)} %fusion.19), custom_call_target="Cholesky" | custom-call | tf_op jit(solution)/shard_map/jit(cholesky)/cholesky | solution.py:12
  444.3 0.6 compare_reduce_fusion
  444.9 0.7 fusion.17
  445.6 7.4 %custom-call.11 = f32[1,96,96]{1,2,0:T(8,128)S(1)} custom-call(f32[1,96,96]{2,1,0:T(8,128)S(1)} %fusion.17), custom_call_target="InvertDiagBlocksLowerTriangular" | custom-call | tf_op jit(solution)/shard_map/triangular_solve/custom-call.0 | solution.py:13
  452.9 0.4 convolution_bitcast_fusion.1
  453.4 0.0 copy-start.4
  453.4 1.3 fusion.11
  454.7 0.0 reduce-scatter.2.cloned.1.call-update
  454.7 21.0 %reduce-scatter.2.cloned.1.call-done = f32[24,8,96]{2,0,1:T(8,128)} async-done(((f32[96,8,96]{2,0,1:T(8,128)}), f32[24,8,96]{2,0,1:T(8,128)}) %reduce-scatter.2.cloned.1.call-update) | async-done | bytes 73744 | tf_op jit(solution)/shard_map/reduce_scatter | solution.py:39
  475.7 1.6 copy.27
  477.3 0.0 copy-done.4
  (9 shorter events, 0.2 us)
Async XLA Ops:
  7.2 170.9 %copy-start = (f32[672,96]{0,1:T(8,128)S(1)}, f32[672,96]{0,1:T(8,128)}, u32[]{:S(2)}) copy-start(f32[672,96]{0,1:T(8,128)} %param.7) | copy-start | bytes 774148
  7.2 170.9 %all-reduce.4.cloned.1.call-start = ((), (), s32[]{:S(2)}) async-start(), calls=%async_computation.2 | async-start | bytes 4128768 | tf_op jit(solution)/shard_map/psum | solution.py:27
  25.3 324.9 %all-reduce.6.cloned.1.call-start = ((), (), s32[]{:S(2)}) async-start(), calls=%async_computation.3 | async-start | bytes 4128768 | tf_op jit(solution)/shard_map/psum | solution.py:32
  178.1 22.1 %copy-start.2 = (f32[672,672]{1,0:T(8,128)S(1)}, f32[672,672]{1,0:T(8,128)}, u32[]{:S(2)}) copy-start(f32[672,672]{1,0:T(8,128)} %all-reduce.4.cloned.1.call-done) | copy-start | bytes 5419012
  220.6 6.5 %copy-start.3 = (f32[96,672]{1,0:T(8,128)}, f32[96,672]{1,0:T(8,128)S(1)}, u32[]{:S(2)}) copy-start(f32[96,672]{1,0:T(8,128)S(1)} %fusion.22) | copy-start | bytes 774148
  245.3 165.5 %all-reduce.8.cloned.1.call-start = ((), (), s32[]{:S(2)}) async-start(), calls=%async_computation.4 | async-start | bytes 4128768 | tf_op jit(solution)/shard_map/psum | solution.py:32
  350.3 125.4 %reduce-scatter.2.cloned.1.call-start = ((), (), s32[]{:S(2)}) async-start(), calls=%async_computation.5 | async-start | bytes 491520 | tf_op jit(solution)/shard_map/reduce_scatter | solution.py:39
  410.8 22.1 %copy-start.1 = (f32[672,672]{1,0:T(8,128)S(1)}, f32[672,672]{1,0:T(8,128)}, u32[]{:S(2)}) copy-start(f32[672,672]{1,0:T(8,128)} %all-reduce.8.cloned.1.call-done) | copy-start | bytes 5419012
  453.4 23.9 %copy-start.4 = (f32[672,96]{0,1:T(8,128)}, f32[672,96]{0,1:T(8,128)S(1)}, u32[]{:S(2)}) copy-start(f32[672,96]{0,1:T(8,128)S(1)} %convolution_bitcast_fusion.1) | copy-start | bytes 774148
Sparse Core Ops, SparseCore 0:
  25.5 152.5 all-reduce.3
  245.5 104.7 all-reduce.5
  352.6 58.1 all-reduce.7
  454.8 20.8 reduce-scatter.1
